TPU v7x, 256 devices: a whole 4x4x8 slice. The times are simulated.
256 devices in a mesh: param: 16 (over x, y), space: 2 (over core), term: 8 (over z).
Axes of the slice: x: 4, y: 4, z: 8, core: 2. Of those that a mesh axis runs over, the one named last changes fastest.
Arguments:
- fields: float32 [128, 2, 8, 128, 128], P('param', None, None, 'space'), may hold values from -4 to 4
- library: int32 [168, 4], P('term'), may hold values from 0 to 6, as said below
- centers_x: int32 [16], replicated, may hold values from 0 to 127
- centers_y: int32 [16], replicated, may hold values from 0 to 127
- centers_t: int32 [4], replicated, may hold values from 0 to 7
- groups: int32 [168], replicated, may hold values from 0 to 23
Outputs:
- coefficients: float32 [128, 2, 168], P(('param', 'term'))
- misfit: float32 [128, 2, 168], P(('param', 'term'))
Inputs may be any that keep to these rules, and one draw needn't show every extreme that they name: `library`: each row (a, b, dx, dy) gives powers a and b of 0 to 6 and derivative orders dx and dy of 0 to 2; rows are distinct, and a = b = 0 only with dx = dy = 0.
All inputs are finite; a program needn't handle non-finite values.
Results may differ from a plain program's by a relative error of at most 0.00011.
Values sent between devices are 32-bit elements; how exact they have to be, the bound alone decides.
A program may use at most 64 MiB of HBM per device.

v0:
```python
import jax
import jax.numpy as jnp
from jax import lax
from jax.sharding import PartitionSpec as P

NX = 128
NY = 128
NT = 8
POWERS = 7
TERMS = 168
TESTS = 1024
RX = 16
RT = 4
GROUPS = 24
highest = lax.Precision.HIGHEST


def space_table(centers, first_row, row_count, extent):
    cell_index = first_row + jnp.arange(row_count, dtype=jnp.int32)
    offset = (cell_index[None, :] - centers[:, None] + extent // 2) % extent - extent // 2
    scaled = offset.astype(jnp.float32) / RX
    bump_base = 1.0 - scaled * scaled
    inside = jnp.abs(scaled) < 1.0
    cube = bump_base * bump_base * bump_base
    bump_value = jnp.where(inside, cube * bump_base, 0.0)
    bump_first = jnp.where(inside, 8.0 * scaled * cube / RX, 0.0)
    bump_second = jnp.where(
        inside, -8.0 * (cube - 6.0 * scaled * scaled * bump_base * bump_base) / (RX * RX), 0.0
    )
    return jnp.stack([bump_value, bump_first, bump_second])


def time_table(centers):
    step_index = jnp.arange(NT, dtype=jnp.int32)
    scaled = (step_index[None, :] - centers[:, None]).astype(jnp.float32) / RT
    bump_base = 1.0 - scaled * scaled
    inside = jnp.abs(scaled) < 1.0
    time_bump = jnp.where(inside, bump_base * bump_base, 0.0)
    time_slope = jnp.where(inside, 4.0 * scaled * bump_base / RT, 0.0)
    return (time_bump, time_slope)


def normalize(gram_matrix):
    diagonal = jnp.diagonal(gram_matrix, axis1=1, axis2=2)
    row_scale = jnp.sqrt(diagonal / TESTS + 1e-06)
    term_scale = row_scale[:, :TERMS]
    correlation = gram_matrix[:, :TERMS, :TERMS] / (
        TESTS * term_scale[:, :, None] * term_scale[:, None, :]
    )
    right_side = gram_matrix[:, TERMS:, :TERMS] / (
        TESTS * term_scale[:, None, :] * row_scale[:, TERMS:, None]
    )
    frobenius = jnp.sqrt(jnp.sum(correlation * correlation, axis=(1, 2)))
    return (correlation, right_side, frobenius)


def group_squares(values, onehot):
    return jnp.dot(jnp.sum(values * values, axis=(0, 1)), onehot, precision=highest)


def shrink(values, totals, onehot):
    threshold = 0.7 * jnp.sqrt(jnp.mean(totals))
    per_term = jnp.dot(onehot, totals, precision=highest)
    factor = jnp.maximum(0.0, 1.0 - threshold / jnp.sqrt(per_term + 1e-12))
    return values * factor


def correlate(correlation, values):
    return jnp.einsum("pij,psj->psi", correlation, values, precision=highest)


def body(fields, library, centers_x, centers_y, centers_t, groups):
    pgroup = fields.shape[0]
    tile_rows = fields.shape[3]
    space_count = lax.axis_size("space")
    term_count = lax.axis_size("term")
    local_terms = library.shape[0]
    row_count = local_terms + 2
    half_tests = TESTS // space_count
    y_table = space_table(centers_y, 0, NY, NY)
    time_bump, time_slope = time_table(centers_t)
    x_table = space_table(centers_x, lax.axis_index("space") * tile_rows, tile_rows, NX)
    share_rows = tile_rows // term_count
    share_start = lax.axis_index("term") * share_rows
    x_share = lax.dynamic_slice_in_dim(x_table[0], share_start, share_rows, 1)
    power_a = library[:, 0]
    power_b = library[:, 1]
    orders = jnp.arange(3, dtype=jnp.int32)
    pick_x = (library[:, 2][:, None] == orders[None, :]).astype(jnp.float32)
    pick_y = (library[:, 3][:, None] == orders[None, :]).astype(jnp.float32)
    x_pick = jnp.einsum("jd,dlx->jlx", pick_x, x_table, precision=highest)
    y_pick = jnp.einsum("jd,dky->jky", pick_y, y_table, precision=highest)

    def tile_integrals(field_pair):
        species_u = field_pair[0]
        species_v = field_pair[1]
        power_u = jnp.ones((local_terms,) + species_u.shape, jnp.float32)
        power_v = jnp.ones((local_terms,) + species_v.shape, jnp.float32)
        for degree in range(1, POWERS):
            power_u = power_u * jnp.where(
                power_a[:, None, None, None] >= degree, species_u[None], 1.0
            )
            power_v = power_v * jnp.where(
                power_b[:, None, None, None] >= degree, species_v[None], 1.0
            )
        monomial = power_u * power_v
        across_y = jnp.einsum("jtxy,jky->jtxk", monomial, y_pick, precision=highest)
        across_t = jnp.einsum("jtxk,rt->jrxk", across_y, time_bump, precision=highest)
        features = jnp.einsum("jrxk,jlx->jrkl", across_t, x_pick, precision=highest).reshape(
            local_terms, TESTS
        )
        share = lax.dynamic_slice_in_dim(field_pair, share_start, share_rows, 2)
        target_y = jnp.einsum("stxy,ky->stxk", share, y_table[0], precision=highest)
        targets = jnp.einsum(
            "stxk,rt,lx->srkl", target_y, time_slope, x_share, precision=highest
        ).reshape(2, TESTS)
        joined = jnp.concatenate([features, targets], axis=0).reshape(
            row_count, space_count, half_tests
        )
        return jnp.swapaxes(joined, 0, 1)

    def fill_param(index, buffer):
        field_pair = lax.dynamic_index_in_dim(fields, index, 0, keepdims=False)
        return lax.dynamic_update_slice_in_dim(
            buffer, tile_integrals(field_pair)[:, None], index, 1
        )

    buffer = jnp.zeros((space_count, pgroup, row_count, half_tests), jnp.float32)
    buffer = lax.fori_loop(0, pgroup, fill_param, buffer)
    received = lax.all_to_all(
        buffer.reshape(space_count * pgroup, row_count, half_tests),
        ("space", "term"),
        split_axis=0,
        concat_axis=1,
        tiled=True,
    )
    blocks = jnp.sum(received.reshape(space_count, term_count, row_count, half_tests), axis=0)
    features_half = blocks[:, :local_terms].reshape(term_count * local_terms, half_tests)
    targets_half = jnp.sum(blocks[:, local_terms:], axis=0)
    half_rows = jnp.concatenate([features_half, targets_half], axis=0)
    whole_rows = lax.all_gather(half_rows, "space", axis=1, tiled=True)
    gram_matrix = jnp.dot(whole_rows, whole_rows.T, precision=highest)[None]
    correlation, right_side, frobenius = normalize(gram_matrix)
    onehot = (groups[:, None] == jnp.arange(GROUPS, dtype=jnp.int32)[None, :]).astype(jnp.float32)
    largest = lax.pmax(jnp.max(frobenius), ("param", "term"))
    step_size = 1.0 / largest
    first_guess = step_size * right_side
    first_sq = lax.psum(group_squares(first_guess, onehot), ("param", "term"))
    first = shrink(first_guess, first_sq, onehot)
    second_guess = first - step_size * (correlate(correlation, first) - right_side)
    second_sq = lax.psum(group_squares(second_guess, onehot), ("param", "term"))
    second = shrink(second_guess, second_sq, onehot)
    coefficients = second / step_size
    misfit = right_side - correlate(correlation, second)
    return (coefficients, misfit)


def solution(mesh):
    return jax.shard_map(
        body,
        mesh=mesh,
        in_specs=(P("param", None, None, "space", None), P("term", None), P(), P(), P(), P()),
        out_specs=(P(("param", "term"), None, None), P(("param", "term"), None, None)),
        check_vma=False,
    )
```

profile of v0, /device:TPU:0, one launch (start us, length us, event | category | flops | bytes accessed | tf_op | source)
XLA Modules:
  0.0 1257.9 jit_solution(2309411352389409611)
XLA Ops:
  0.6 0.8 multiply_select_fusion.2
  1.5 0.7 fusion.127
  2.2 0.8 slice_bitcast_fusion.1
  3.4 0.8 multiply_select_fusion.5
  4.6 175.0 %while.18 = (s32[]{:T(128)}, f32[2,8,23,512]{3,0,2,1:T(2,128)S(1)}, s32[21,1]{0,1:T(1,128)S(1)}, f32[8,2,8,64,128]{4,3,2,1,0:T(8,128)}, s32[21,1]{0,1:T(1,128)S(...) while((s32[]{:T(128)}, f32[2,8,23,512]{3,0,2,1:T(2,128)S(1)}, ...), condition=%wide.region_1.2_spmd.clone.clone, body=%wide.region_0.1_spmd.clone.clone.sunk | while | flops 324181856 | bytes 4605749 | solution.py:129
  4.6 1.1 dynamic-slice_bitcast_fusion.6
  5.7 16.0 %fusion.203 = f32[21,8,64,16]{2,3,1,0:T(8,128)S(1)} fusion(f32[8,64,128]{2,1,0:T(8,128)S(1)} %get-tuple-element.566, f32[8,64,128]{2,1,0:T(8,128)S(1)} %get-tuple-element.567, pred[21]{0:T(512)(128)(4,1)S(1)} %get-tuple-element.568, pred[21]{0:T(512)(128)(4,1)S(1)} %get-tuple-element.569, pred[21]{0:T(512)(128)(4,1)S(1)} %get-tuple-element.570, ...), kind=kOutput, calls=%fused_computation.4.clone.1 | convolution fusion | flops 295895040 | bytes 1384700 | tf_op jit(solution)/shard_map/while/body/eval_jaxpr/jtxy,jky->jtxk/dot_general | solution.py:107
  21.7 1.6 fusion.204
  24.5 0.9 dynamic-slice_bitcast_fusion.5
  26.5 1.1 dynamic-slice_bitcast_fusion.6
  27.6 16.0 %fusion.203 = f32[21,8,64,16]{2,3,1,0:T(8,128)S(1)} fusion(f32[8,64,128]{2,1,0:T(8,128)S(1)} %get-tuple-element.566, f32[8,64,128]{2,1,0:T(8,128)S(1)} %get-tuple-element.567, pred[21]{0:T(512)(128)(4,1)S(1)} %get-tuple-element.568, pred[21]{0:T(512)(128)(4,1)S(1)} %get-tuple-element.569, pred[21]{0:T(512)(128)(4,1)S(1)} %get-tuple-element.570, ...), kind=kOutput, calls=%fused_computation.4.clone.1 | convolution fusion | flops 295895040 | bytes 1384700 | tf_op jit(solution)/shard_map/while/body/eval_jaxpr/jtxy,jky->jtxk/dot_general | solution.py:107
  43.6 1.6 fusion.204
  46.3 0.9 dynamic-slice_bitcast_fusion.5
  48.3 1.1 dynamic-slice_bitcast_fusion.6
  49.4 16.0 %fusion.203 = f32[21,8,64,16]{2,3,1,0:T(8,128)S(1)} fusion(f32[8,64,128]{2,1,0:T(8,128)S(1)} %get-tuple-element.566, f32[8,64,128]{2,1,0:T(8,128)S(1)} %get-tuple-element.567, pred[21]{0:T(512)(128)(4,1)S(1)} %get-tuple-element.568, pred[21]{0:T(512)(128)(4,1)S(1)} %get-tuple-element.569, pred[21]{0:T(512)(128)(4,1)S(1)} %get-tuple-element.570, ...), kind=kOutput, calls=%fused_computation.4.clone.1 | convolution fusion | flops 295895040 | bytes 1384700 | tf_op jit(solution)/shard_map/while/body/eval_jaxpr/jtxy,jky->jtxk/dot_general | solution.py:107
  65.4 1.6 fusion.204
  68.2 0.9 dynamic-slice_bitcast_fusion.5
  70.2 1.1 dynamic-slice_bitcast_fusion.6
  71.3 16.0 %fusion.203 = f32[21,8,64,16]{2,3,1,0:T(8,128)S(1)} fusion(f32[8,64,128]{2,1,0:T(8,128)S(1)} %get-tuple-element.566, f32[8,64,128]{2,1,0:T(8,128)S(1)} %get-tuple-element.567, pred[21]{0:T(512)(128)(4,1)S(1)} %get-tuple-element.568, pred[21]{0:T(512)(128)(4,1)S(1)} %get-tuple-element.569, pred[21]{0:T(512)(128)(4,1)S(1)} %get-tuple-element.570, ...), kind=kOutput, calls=%fused_computation.4.clone.1 | convolution fusion | flops 295895040 | bytes 1384700 | tf_op jit(solution)/shard_map/while/body/eval_jaxpr/jtxy,jky->jtxk/dot_general | solution.py:107
  87.3 1.6 fusion.204
  90.0 0.9 dynamic-slice_bitcast_fusion.5
  92.1 1.1 dynamic-slice_bitcast_fusion.6
  93.1 16.0 %fusion.203 = f32[21,8,64,16]{2,3,1,0:T(8,128)S(1)} fusion(f32[8,64,128]{2,1,0:T(8,128)S(1)} %get-tuple-element.566, f32[8,64,128]{2,1,0:T(8,128)S(1)} %get-tuple-element.567, pred[21]{0:T(512)(128)(4,1)S(1)} %get-tuple-element.568, pred[21]{0:T(512)(128)(4,1)S(1)} %get-tuple-element.569, pred[21]{0:T(512)(128)(4,1)S(1)} %get-tuple-element.570, ...), kind=kOutput, calls=%fused_computation.4.clone.1 | convolution fusion | flops 295895040 | bytes 1384700 | tf_op jit(solution)/shard_map/while/body/eval_jaxpr/jtxy,jky->jtxk/dot_general | solution.py:107
  109.1 1.6 fusion.204
  110.8 0.7 fusion.205
  111.9 0.9 dynamic-slice_bitcast_fusion.5
  113.9 1.1 dynamic-slice_bitcast_fusion.6
  115.0 16.0 %fusion.203 = f32[21,8,64,16]{2,3,1,0:T(8,128)S(1)} fusion(f32[8,64,128]{2,1,0:T(8,128)S(1)} %get-tuple-element.566, f32[8,64,128]{2,1,0:T(8,128)S(1)} %get-tuple-element.567, pred[21]{0:T(512)(128)(4,1)S(1)} %get-tuple-element.568, pred[21]{0:T(512)(128)(4,1)S(1)} %get-tuple-element.569, pred[21]{0:T(512)(128)(4,1)S(1)} %get-tuple-element.570, ...), kind=kOutput, calls=%fused_computation.4.clone.1 | convolution fusion | flops 295895040 | bytes 1384700 | tf_op jit(solution)/shard_map/while/body/eval_jaxpr/jtxy,jky->jtxk/dot_general | solution.py:107
  131.0 1.6 fusion.204
  133.7 0.9 dynamic-slice_bitcast_fusion.5
  135.8 1.1 dynamic-slice_bitcast_fusion.6
  136.9 16.0 %fusion.203 = f32[21,8,64,16]{2,3,1,0:T(8,128)S(1)} fusion(f32[8,64,128]{2,1,0:T(8,128)S(1)} %get-tuple-element.566, f32[8,64,128]{2,1,0:T(8,128)S(1)} %get-tuple-element.567, pred[21]{0:T(512)(128)(4,1)S(1)} %get-tuple-element.568, pred[21]{0:T(512)(128)(4,1)S(1)} %get-tuple-element.569, pred[21]{0:T(512)(128)(4,1)S(1)} %get-tuple-element.570, ...), kind=kOutput, calls=%fused_computation.4.clone.1 | convolution fusion | flops 295895040 | bytes 1384700 | tf_op jit(solution)/shard_map/while/body/eval_jaxpr/jtxy,jky->jtxk/dot_general | solution.py:107
  152.8 1.6 fusion.204
  155.6 0.9 dynamic-slice_bitcast_fusion.5
  157.6 1.1 dynamic-slice_bitcast_fusion.6
  158.7 16.0 %fusion.203 = f32[21,8,64,16]{2,3,1,0:T(8,128)S(1)} fusion(f32[8,64,128]{2,1,0:T(8,128)S(1)} %get-tuple-element.566, f32[8,64,128]{2,1,0:T(8,128)S(1)} %get-tuple-element.567, pred[21]{0:T(512)(128)(4,1)S(1)} %get-tuple-element.568, pred[21]{0:T(512)(128)(4,1)S(1)} %get-tuple-element.569, pred[21]{0:T(512)(128)(4,1)S(1)} %get-tuple-element.570, ...), kind=kOutput, calls=%fused_computation.4.clone.1 | convolution fusion | flops 295895040 | bytes 1384700 | tf_op jit(solution)/shard_map/while/body/eval_jaxpr/jtxy,jky->jtxk/dot_general | solution.py:107
  174.7 1.6 fusion.204
  177.5 0.9 dynamic-slice_bitcast_fusion.5
  179.6 1.0 copy.33
  180.7 7.0 all-to-all-start
  187.6 20.5 %all-to-all-done = f32[16,23,512]{2,1,0:T(8,128)S(1)} async-done(((f32[16,23,512]{2,1,0:T(8,128)}), f32[16,23,512]{2,1,0:T(8,128)S(1)}, u32[]{:S(2)}, u32[]{:S(2)}) %all-to-all-start) | async-done | bytes 753696 | tf_op jit(solution)/shard_map/all_to_all | solution.py:130
  208.4 3.0 all_gather.3
  211.4 0.7 fusion.167
  212.2 2.8 gather_fusion
  216.5 349.0 %pmax.7 = f32[]{:T(128)} all-reduce(f32[]{:T(128)S(6)} %sqrt.28), channel_id=1, replica_groups=mesh['param'=16,'space'=2,'term'=8] {'param','term'}, use_global_device_ids=true, to_apply=%region_5.6 | all-reduce | flops 1 | bytes 8 | tf_op jit(solution)/shard_map/pmax | solution.py:145
  566.5 342.2 %psum.14 = f32[24]{0:T(128)S(1)} all-reduce(f32[24]{0:T(128)S(1)} %convolution_bitcast_fusion.5), channel_id=1, replica_groups=mesh['param'=16,'space'=2,'term'=8] {'param','term'}, use_global_device_ids=true, to_apply=%region_7.8 | all-reduce | flops 24 | bytes 192 | tf_op jit(solution)/shard_map/psum | solution.py:148
  910.7 344.2 %psum.15 = f32[24]{0:T(128)S(1)} all-reduce(f32[24]{0:T(128)S(1)} %convolution_bitcast_fusion.4), channel_id=1, replica_groups=mesh['param'=16,'space'=2,'term'=8] {'param','term'}, use_global_device_ids=true, to_apply=%region_10.11 | all-reduce | flops 24 | bytes 192 | tf_op jit(solution)/shard_map/psum | solution.py:151
  1256.5 0.8 fusion.112
  (132 shorter events, 21.0 us)
Async XLA Ops:
  5.7 16.0 %copy-start = (s32[4]{0:T(128)S(1)}, s32[4]{0:T(128)}, u32[]{:S(2)}) copy-start(s32[4]{0:T(128)} %get-tuple-element.619) | copy-start | bytes 52 | tf_op jit(solution)/shard_map/while
  21.7 3.7 copy-start.1
  27.6 16.0 %copy-start = (s32[4]{0:T(128)S(1)}, s32[4]{0:T(128)}, u32[]{:S(2)}) copy-start(s32[4]{0:T(128)} %get-tuple-element.619) | copy-start | bytes 52 | tf_op jit(solution)/shard_map/while
  43.5 3.7 copy-start.1
  49.4 16.0 %copy-start = (s32[4]{0:T(128)S(1)}, s32[4]{0:T(128)}, u32[]{:S(2)}) copy-start(s32[4]{0:T(128)} %get-tuple-element.619) | copy-start | bytes 52 | tf_op jit(solution)/shard_map/while
  65.4 3.7 copy-start.1
  71.3 16.0 %copy-start = (s32[4]{0:T(128)S(1)}, s32[4]{0:T(128)}, u32[]{:S(2)}) copy-start(s32[4]{0:T(128)} %get-tuple-element.619) | copy-start | bytes 52 | tf_op jit(solution)/shard_map/while
  87.2 3.7 copy-start.1
  93.1 16.0 %copy-start = (s32[4]{0:T(128)S(1)}, s32[4]{0:T(128)}, u32[]{:S(2)}) copy-start(s32[4]{0:T(128)} %get-tuple-element.619) | copy-start | bytes 52 | tf_op jit(solution)/shard_map/while
  109.1 3.7 copy-start.1
  115.0 16.0 %copy-start = (s32[4]{0:T(128)S(1)}, s32[4]{0:T(128)}, u32[]{:S(2)}) copy-start(s32[4]{0:T(128)} %get-tuple-element.619) | copy-start | bytes 52 | tf_op jit(solution)/shard_map/while
  131.0 3.7 copy-start.1
  136.8 16.0 %copy-start = (s32[4]{0:T(128)S(1)}, s32[4]{0:T(128)}, u32[]{:S(2)}) copy-start(s32[4]{0:T(128)} %get-tuple-element.619) | copy-start | bytes 52 | tf_op jit(solution)/shard_map/while
  152.8 3.7 copy-start.1
  158.7 16.0 %copy-start = (s32[4]{0:T(128)S(1)}, s32[4]{0:T(128)}, u32[]{:S(2)}) copy-start(s32[4]{0:T(128)} %get-tuple-element.619) | copy-start | bytes 52 | tf_op jit(solution)/shard_map/while
  174.7 3.7 copy-start.1
  180.7 385.7 %copy-start.2 = (s32[168]{0:T(256)S(1)}, s32[168]{0:T(256)}, u32[]{:S(2)}) copy-start(s32[168]{0:T(256)} %param.13) | copy-start | bytes 2020
  180.7 27.5 %all-to-all-start = ((f32[16,23,512]{2,1,0:T(8,128)}), f32[16,23,512]{2,1,0:T(8,128)S(1)}, u32[]{:S(2)}, u32[]{:S(2)}) async-start(f32[16,23,512]{2,1,0:T(8,128)} %bitcast.5), calls=%async_computation | async-start | bytes 1572864 | tf_op jit(solution)/shard_map/all_to_all | solution.py:130
where the time goes:
time: 1260 us
  blocking collectives  1040 us (83%)
  matrix products  157 us (12%)
  local copies, waits for them, and re-layouts  24.8 us (2%)
  waiting for transfers between devices  20.5 us (2%)
    pmax x1, blocking collectives, body(): largest = lax.pmax(jnp.max(frobenius), ('param', 'term'))  349 us
    psum x1, blocking collectives, body(): second_sq = lax.psum(group_squares(second_guess, onehot), ('param', 'term'))  344 us
    psum x1, blocking collectives, body(): first_sq = lax.psum(group_squares(first_guess, onehot), ('param', 'term'))  342 us
    dot_general x8, matrix products, tile_integrals(): across_y = jnp.einsum('jtxy,jky->jtxk', monomial, y_pick, precision=highest)  128 us
  transfers between devices with their start and end apart: 1, of which 1 were waited for; matrix products, arithmetic and copies ran while one was open for 0% of the time, Pallas kernels for 0%

commit v1 on v0

--- a/solution.py
+++ b/solution.py
@@ -145,7 +145,9 @@
     largest = lax.pmax(jnp.max(frobenius), ("param", "term"))
     step_size = 1.0 / largest
     first_guess = step_size * right_side
-    first_sq = lax.psum(group_squares(first_guess, onehot), ("param", "term"))
+    part = group_squares(first_guess, onehot)
+    parts = lax.all_gather(part, ("param", "term"))
+    first_sq = jnp.sum(parts, axis=0)
     first = shrink(first_guess, first_sq, onehot)
     second_guess = first - step_size * (correlate(correlation, first) - right_side)
     second_sq = lax.psum(group_squares(second_guess, onehot), ("param", "term"))

time: 1260 us -> 1600 us (1.27)
  blocking collectives: 1040 us -> 1380 us
    unnamed x0 -> x1, blocking collectives: none -> 682 us
    psum x1 -> x0, blocking collectives: 342 us -> none  [body(): first_sq = lax.psum(group_squares(first_guess, onehot), ('param', 'term'))]
where the time goes in v1:
time: 1600 us
  blocking collectives  1380 us (86%)
  matrix products  157 us (10%)
  local copies, waits for them, and re-layouts  25.7 us (2%)
  waiting for transfers between devices  19.3 us (1%)
    unnamed x1, blocking collectives  682 us
    pmax x1, blocking collectives, body(): largest = lax.pmax(jnp.max(frobenius), ('param', 'term'))  349 us
    psum x1, blocking collectives, body(): second_sq = lax.psum(group_squares(second_guess, onehot), ('param', 'term'))  342 us
    dot_general x8, matrix products, tile_integrals(): across_y = jnp.einsum('jtxy,jky->jtxk', monomial, y_pick, precision=highest)  128 us
  transfers between devices with their start and end apart: 1, of which 1 were waited for; matrix products, arithmetic and copies ran while one was open for 0% of the time, Pallas kernels for 0%

profile of v1, /device:TPU:0, one launch (start us, length us, event | category | flops | bytes accessed | tf_op | source)
XLA Modules:
  0.0 1595.7 jit_solution(12817031866487683375)
XLA Ops:
  0.6 0.8 multiply_select_fusion.2
  1.5 0.7 fusion.127
  2.2 0.8 slice_bitcast_fusion.1
  3.4 0.8 multiply_select_fusion.5
  4.6 175.0 %while.18 = (s32[]{:T(128)}, f32[2,8,23,512]{3,0,2,1:T(2,128)S(1)}, s32[21,1]{0,1:T(1,128)S(1)}, f32[8,2,8,64,128]{4,3,2,1,0:T(8,128)}, s32[21,1]{0,1:T(1,128)S(...) while((s32[]{:T(128)}, f32[2,8,23,512]{3,0,2,1:T(2,128)S(1)}, ...), condition=%wide.region_1.2_spmd.clone.clone, body=%wide.region_0.1_spmd.clone.clone.sunk | while | flops 324181856 | bytes 4605749 | solution.py:129
  4.6 1.1 dynamic-slice_bitcast_fusion.6
  5.7 16.0 fusion.203
  21.7 1.6 fusion.204
  24.5 0.9 dynamic-slice_bitcast_fusion.5
  26.5 1.1 dynamic-slice_bitcast_fusion.6
  27.6 16.0 fusion.203
  43.6 1.6 fusion.204
  45.2 0.7 fusion.205
  46.3 0.9 dynamic-slice_bitcast_fusion.5
  48.4 1.1 dynamic-slice_bitcast_fusion.6
  49.4 16.0 fusion.203
  65.4 1.6 fusion.204
  68.2 0.9 dynamic-slice_bitcast_fusion.5
  70.2 1.1 dynamic-slice_bitcast_fusion.6
  71.3 16.0 fusion.203
  87.3 1.6 fusion.204
  90.0 0.9 dynamic-slice_bitcast_fusion.5
  92.1 1.1 dynamic-slice_bitcast_fusion.6
  93.2 16.0 fusion.203
  109.1 1.6 fusion.204
  111.9 0.9 dynamic-slice_bitcast_fusion.5
  113.9 1.1 dynamic-slice_bitcast_fusion.6
  115.0 16.0 fusion.203
  131.0 1.6 fusion.204
  133.8 0.9 dynamic-slice_bitcast_fusion.5
  135.8 1.1 dynamic-slice_bitcast_fusion.6
  136.9 16.0 fusion.203
  152.8 1.6 fusion.204
  155.6 0.9 dynamic-slice_bitcast_fusion.5
  157.6 1.1 dynamic-slice_bitcast_fusion.6
  158.7 16.0 fusion.203
  174.7 1.6 fusion.204
  177.5 0.9 dynamic-slice_bitcast_fusion.5
  179.6 1.0 copy.33
  180.7 7.0 all-to-all-start
  188.9 19.3 %all-to-all-done = f32[16,23,512]{2,1,0:T(8,128)S(1)} async-done(((f32[16,23,512]{2,1,0:T(8,128)}), f32[16,23,512]{2,1,0:T(8,128)S(1)}, u32[]{:S(2)}, u32[]{:S(2)}) %all-to-all-start) | async-done | bytes 753696 | tf_op jit(solution)/shard_map/all_to_all | solution.py:130
  208.4 3.0 all_gather.9
  211.4 0.7 fusion.167
  212.2 2.8 gather_fusion
  216.5 349.0 %pmax.7 = f32[]{:T(128)} all-reduce(f32[]{:T(128)S(6)} %sqrt.28), channel_id=1, replica_groups=mesh['param'=16,'space'=2,'term'=8] {'param','term'}, use_global_device_ids=true, to_apply=%region_5.6 | all-reduce | flops 1 | bytes 8 | tf_op jit(solution)/shard_map/pmax | solution.py:145
  566.8 681.6 %all-reduce = f32[3072]{0:T(1024)S(1)} all-reduce(f32[3072]{0:T(1024)S(1)} %dynamic-update-slice), channel_id=2, replica_groups=mesh['param'=16,'space'=2,'term'=8] {'param','term'}, use_global_device_ids=true, to_apply=%add | all-reduce | flops 3072 | bytes 24576
  1250.5 342.2 %psum.7 = f32[24]{0:T(128)S(1)} all-reduce(f32[24]{0:T(128)S(1)} %convolution_bitcast_fusion.4), channel_id=1, replica_groups=mesh['param'=16,'space'=2,'term'=8] {'param','term'}, use_global_device_ids=true, to_apply=%region_10.11 | all-reduce | flops 24 | bytes 192 | tf_op jit(solution)/shard_map/psum | solution.py:153
  1594.3 0.8 fusion.112
  (139 shorter events, 21.9 us)
Async XLA Ops:
  4.6 183.1 %copy-start.3 = (u32[256]{0:T(256)S(1)}, u32[256]{0:T(256)}, u32[]{:S(2)}) copy-start(u32[256]{0:T(256)} %constant.300) | copy-start | bytes 3076
  5.7 16.0 %copy-start = (s32[4]{0:T(128)S(1)}, s32[4]{0:T(128)}, u32[]{:S(2)}) copy-start(s32[4]{0:T(128)} %get-tuple-element.619) | copy-start | bytes 52 | tf_op jit(solution)/shard_map/while
  21.7 3.7 copy-start.1
  27.6 16.0 %copy-start = (s32[4]{0:T(128)S(1)}, s32[4]{0:T(128)}, u32[]{:S(2)}) copy-start(s32[4]{0:T(128)} %get-tuple-element.619) | copy-start | bytes 52 | tf_op jit(solution)/shard_map/while
  43.5 3.7 copy-start.1
  49.4 16.0 %copy-start = (s32[4]{0:T(128)S(1)}, s32[4]{0:T(128)}, u32[]{:S(2)}) copy-start(s32[4]{0:T(128)} %get-tuple-element.619) | copy-start | bytes 52 | tf_op jit(solution)/shard_map/while
  65.4 3.7 copy-start.1
  71.3 16.0 %copy-start = (s32[4]{0:T(128)S(1)}, s32[4]{0:T(128)}, u32[]{:S(2)}) copy-start(s32[4]{0:T(128)} %get-tuple-element.619) | copy-start | bytes 52 | tf_op jit(solution)/shard_map/while
  87.3 3.7 copy-start.1
  93.1 16.0 %copy-start = (s32[4]{0:T(128)S(1)}, s32[4]{0:T(128)}, u32[]{:S(2)}) copy-start(s32[4]{0:T(128)} %get-tuple-element.619) | copy-start | bytes 52 | tf_op jit(solution)/shard_map/while
  109.1 3.7 copy-start.1
  115.0 16.0 %copy-start = (s32[4]{0:T(128)S(1)}, s32[4]{0:T(128)}, u32[]{:S(2)}) copy-start(s32[4]{0:T(128)} %get-tuple-element.619) | copy-start | bytes 52 | tf_op jit(solution)/shard_map/while
  131.0 3.7 copy-start.1
  136.9 16.0 %copy-start = (s32[4]{0:T(128)S(1)}, s32[4]{0:T(128)}, u32[]{:S(2)}) copy-start(s32[4]{0:T(128)} %get-tuple-element.619) | copy-start | bytes 52 | tf_op jit(solution)/shard_map/while
  152.8 3.7 copy-start.1
  158.7 16.0 %copy-start = (s32[4]{0:T(128)S(1)}, s32[4]{0:T(128)}, u32[]{:S(2)}) copy-start(s32[4]{0:T(128)} %get-tuple-element.619) | copy-start | bytes 52 | tf_op jit(solution)/shard_map/while
  174.7 3.7 copy-start.1
  180.7 385.7 %copy-start.2 = (s32[168]{0:T(256)S(1)}, s32[168]{0:T(256)}, u32[]{:S(2)}) copy-start(s32[168]{0:T(256)} %param.13) | copy-start | bytes 2020
  180.7 27.5 %all-to-all-start = ((f32[16,23,512]{2,1,0:T(8,128)}), f32[16,23,512]{2,1,0:T(8,128)S(1)}, u32[]{:S(2)}, u32[]{:S(2)}) async-start(f32[16,23,512]{2,1,0:T(8,128)} %bitcast.5), calls=%async_computation | async-start | bytes 1572864 | tf_op jit(solution)/shard_map/all_to_all | solution.py:130
